TPU v7x, 32 devices: a whole 2x2x4 slice. The times are simulated.
32 devices in a mesh: freq: 4 (over z), bl: 8 (over y, x, core).
Axes of the slice: x: 2, y: 2, z: 4, core: 2. Of those that a mesh axis runs over, the one named last changes fastest.
Arguments:
- vis: float32 [2, 128, 16384], P(None, 'freq', 'bl'), may hold values from -60 to 60
- coherency: bfloat16 [2, 4, 128, 16384], P(None, None, 'freq', 'bl'), may hold values from -6 to 6
- gains_init: float32 [2, 4, 128, 512], P(None, None, 'freq', 'bl'), may hold values from -4 to 4
- station_pairs: int32 [2, 16384], P(None, 'bl'), may hold values from 0 to 511, as said below
Outputs:
- gains: float32 [2, 4, 128, 512], P(None, None, 'freq', 'bl')
- consensus: float32 [2, 4, 128, 512], P(None, None, 'freq', 'bl')
Inputs may be any that keep to these rules, and one draw needn't show every extreme that they name: `station_pairs`: in each column the two stations differ.
All inputs are finite; a program needn't handle non-finite values.
Results may differ from a plain program's by a relative error of at most 0.0013.
Values may be sent and summed in bfloat16 or wider, within the bound.
A program may use at most 64 MiB of HBM per device.

v0:
```python
import functools

import numpy as np
import jax
import jax.numpy as jnp
from jax import lax
from jax.experimental import pallas as pl
from jax.experimental.pallas import tpu as pltpu
from jax.sharding import PartitionSpec as P

STATION_TOTAL = 512
SKY_DIRECTIONS = 4
ITERS = 2
ROUNDS = 2
JD = 4
MESH = pl.DeviceIdType.MESH
HIGH = lax.Precision.HIGHEST
F32 = jnp.float32
BF16 = jnp.bfloat16
LO = 128
VMEM_CAP = 60 * 1024 * 1024


def basis_rows(channels):
    position = (2.0 * np.arange(channels, dtype=np.float32) + np.float32(1.0)) / np.float32(channels) - np.float32(1.0)
    raw = [np.ones_like(position), position, position * position, position * position * position]
    rows = []
    for vector in raw:
        for other in rows:
            vector = vector - np.sum(other * vector, dtype=np.float32) * other
        rows.append(vector / np.sqrt(np.sum(vector * vector, dtype=np.float32)))
    return np.stack(rows).astype(np.float32)


def greet(axes):
    barrier = pltpu.get_barrier_semaphore()
    count = 0
    for axis in axes:
        n = lax.axis_size(axis)
        me = lax.axis_index(axis)
        for o in range(1, n):
            pl.semaphore_signal(barrier, inc=1, device_id={axis: lax.rem(me + o, n)}, device_id_type=MESH)
            count += 1
    pl.semaphore_wait(barrier, count)


def sum_directions(x, cl):
    rows = x.shape[0]
    dirs = rows // cl
    if cl == 4 and rows == 16:
        half = x[:8] + x[8:]
        half = half + pltpu.roll(half, 4, 0)
        return jnp.concatenate([half, half], axis=0)
    total = x[:cl]
    for d in range(1, dirs):
        total = total + x[d * cl : (d + 1) * cl]
    return jnp.concatenate([total] * dirs, axis=0)


def flip(me, o, n):
    value = 0
    bit = 1
    while bit < n:
        value = value + lax.rem(lax.rem(lax.div(me, bit), 2) + lax.rem(lax.div(o, bit), 2), 2) * bit
        bit *= 2
    return value


def calibrate_kernel(
    n, m, cl, rho,
    coh_in, vis_in, gains_in, pairs_in, wide_ref, basis_ref,
    gains_ref, cons_ref,
    coh_all, vis_all, gains_all, pairs_all, onehot, table, acc,
    part, got, chunk, got_f, whole, coef, fit_out, gains_send, got_b, got_g, chunk_b, got_fb,
    sx, rx, lx, s1, r1, s2, r2, s3, r3, s4, r4, s5, r5,
):
    dirs = SKY_DIRECTIONS
    rows = dirs * cl
    lo = LO
    hi = STATION_TOTAL // lo
    per = vis_in.shape[2]
    owned = STATION_TOTAL // n
    me = lax.axis_index("bl")
    me_f = lax.axis_index("freq")
    greet(("bl", "freq"))

    def transfer(a, o, peer, src, slot):
        ref = (gains_in, pairs_in, coh_in, vis_in)[a]
        dst = (gains_all, pairs_all, coh_all, vis_all)[a]
        return pltpu.make_async_remote_copy(
            ref if a == 1 else ref.at[src], dst.at[slot], sx.at[a, o - 1], rx.at[a, o - 1],
            device_id={"bl": peer}, device_id_type=MESH,
        )

    sends = []
    for group in ((0, 1), (2, 3)):
        for o in range(1, n):
            peer = flip(me, o, n)
            for a in group:
                copy = transfer(a, o, peer, peer, me)
                copy.start()
                sends.append(copy)
    own = [
        pltpu.make_async_copy(gains_in.at[me], gains_all.at[me], lx.at[0]),
        pltpu.make_async_copy(pairs_in, pairs_all.at[me], lx.at[1]),
        pltpu.make_async_copy(coh_in.at[me], coh_all.at[me], lx.at[2]),
        pltpu.make_async_copy(vis_in.at[me], vis_all.at[me], lx.at[3]),
    ]
    for copy in own:
        copy.start()
    for copy in own:
        copy.wait()
    for o in range(1, n):
        transfer(0, o, flip(me, o, n), me, flip(me, o, n)).wait_recv()

    wide = wide_ref[me_f * n + me]

    def build(block):
        station = lax.broadcasted_iota(jnp.int32, (lo, per), 0)
        for t in range(2):
            index = pairs_all[block, t : t + 1, :] & (lo - 1)
            onehot[t, block] = jnp.where(station == index, 1.0, 0.0).astype(BF16)

    def pick(x, group):
        value = x[: 2 * rows]
        for h in range(1, hi):
            value = jnp.where(group == h, x[2 * rows * h : 2 * rows * (h + 1)], value)
        return value

    def spread(terms, group):
        terms = jnp.concatenate(terms, axis=0).astype(BF16)
        return jnp.concatenate(
            [
                terms * jnp.broadcast_to(jnp.where(group == h, 1.0, 0.0), (3 * rows, per)).astype(BF16)
                for h in range(hi)
            ],
            axis=0,
        )

    def add_block(block):
        group0 = lax.shift_right_logical(pairs_all[block, 0:1, :], lo.bit_length() - 1)
        group1 = lax.shift_right_logical(pairs_all[block, 1:2, :], lo.bit_length() - 1)
        ohn = onehot[0, block]
        ohf = onehot[1, block]
        near = pick(jnp.dot(table[...], ohn, preferred_element_type=F32), group0)
        far = pick(jnp.dot(table[...], ohf, preferred_element_type=F32), group1)
        nr, ni = near[:rows], near[rows:]
        fr, fi = far[:rows], far[rows:]
        cr = coh_all[block, 0].astype(F32)
        ci = coh_all[block, 1].astype(F32)
        zr = cr * fr + ci * fi
        zi = ci * fr - cr * fi
        xr = nr * cr - ni * ci
        xi = nr * ci + ni * cr
        mr = sum_directions(nr * zr - ni * zi, cl)
        mi = sum_directions(nr * zi + ni * zr, cl)
        v = vis_all[block]
        rr = jnp.concatenate([v[:cl]] * dirs, axis=0) - mr
        ri = jnp.concatenate([v[cl:]] * dirs, axis=0) - mi
        t1 = spread([rr * zr + ri * zi, ri * zr - rr * zi, zr * zr + zi * zi], group0)
        t2 = spread([rr * xr + ri * xi, rr * xi - ri * xr, xr * xr + xi * xi], group1)
        contract = (((1,), (1,)), ((), ()))
        acc[...] += lax.dot_general(t1, ohn, contract, preferred_element_type=F32) + lax.dot_general(
            t2, ohf, contract, preferred_element_type=F32
        )

    def load_table(gains):
        rounded = gains.astype(BF16)
        table[...] = jnp.concatenate([rounded[:, h * lo : (h + 1) * lo] for h in range(hi)], axis=0)
        acc[...] = jnp.zeros_like(acc)

    def advance(gains, target):
        sums = jnp.concatenate([acc[3 * rows * h : 3 * rows * (h + 1)] for h in range(hi)], axis=1)
        below = 2.0 * sums[2 * rows :] + rho
        below = jnp.concatenate([below, below], axis=0)
        return gains + (sums[: 2 * rows] + rho * (target - gains)) / below

    def again(block, carry):
        add_block(block)
        return carry

    def whole_rows(ref):
        blocks = [ref[s] for s in range(n)]
        return jnp.concatenate(
            [jnp.concatenate([b[:, a * owned : (a + 1) * owned] for b in blocks], axis=1) for a in range(2)], axis=0
        )

    def block_of(x, s):
        half = x.shape[0] // 2
        return jnp.concatenate([x[:half, s * owned : (s + 1) * owned], x[half:, s * owned : (s + 1) * owned]], axis=1)

    def over_freq(src, slots, send, recv):
        copies = []
        for o in range(1, m):
            copy = pltpu.make_async_remote_copy(
                src, slots.at[o - 1], send.at[o - 1], recv.at[o - 1],
                device_id={"freq": lax.rem(me_f + o, m)}, device_id_type=MESH,
            )
            copy.start()
            copies.append(copy)
        total = src[...]
        for o in range(1, m):
            copies[o - 1].wait()
            total = total + slots[o - 1]
        return total

    gains = whole_rows(gains_all)
    target = gains
    load_table(gains)

    def arriving(o, carry):
        peer = flip(me, o, n)
        for a in (1, 2, 3):
            transfer(a, o, peer, me, peer).wait_recv()
        build(peer)
        add_block(peer)
        return carry

    build(me)
    add_block(me)
    lax.fori_loop(1, n, arriving, 0)
    gains = advance(gains, target)
    for _ in range(ITERS - 1):
        load_table(gains)
        lax.fori_loop(0, n, again, 0)
        gains = advance(gains, target)
    for copy in sends:
        copy.wait_send()

    fitted = jnp.dot(wide, gains, precision=HIGH, preferred_element_type=F32)
    for s in range(n):
        part[s] = block_of(fitted, s)
    copies = []
    for o in range(1, n):
        peer = flip(me, o, n)
        copy = pltpu.make_async_remote_copy(
            part.at[peer], got.at[o - 1], s1.at[o - 1], r1.at[o - 1],
            device_id={"bl": peer}, device_id_type=MESH,
        )
        copy.start()
        copies.append(copy)
    total = part[me]
    for o in range(1, n):
        copies[o - 1].wait()
        total = total + got[o - 1]
    chunk[...] = total
    total = over_freq(chunk, got_f, s2, r2)
    whole[...] = total
    copies = []
    for o in range(1, n):
        copy = pltpu.make_async_remote_copy(
            whole, coef.at[me], s3.at[o - 1], r3.at[o - 1],
            device_id={"bl": flip(me, o, n)}, device_id_type=MESH,
        )
        copy.start()
        copies.append(copy)
    coef[me] = total
    for copy in copies:
        copy.wait_send()
    for o in range(1, n):
        peer = flip(me, o, n)
        pltpu.make_async_remote_copy(
            whole, coef.at[peer], s3.at[o - 1], r3.at[o - 1],
            device_id={"bl": peer}, device_id_type=MESH,
        ).wait_recv()

    consensus = lax.dot_general(
        wide, whole_rows(coef), (((0,), (0,)), ((), ())), precision=HIGH, preferred_element_type=F32
    )
    dual = gains - consensus
    target = consensus - dual
    for _ in range(ITERS):
        load_table(gains)
        lax.fori_loop(0, n, again, 0)
        gains = advance(gains, target)

    fitted = jnp.dot(wide, gains + dual, precision=HIGH, preferred_element_type=F32)
    for s in range(n):
        fit_out[s] = block_of(fitted, s)
        gains_send[s] = block_of(gains, s)

    def deliver(k, o, peer, slot):
        src, dst = ((fit_out, got_b), (gains_send, got_g))[k]
        return pltpu.make_async_remote_copy(
            src.at[peer], dst.at[slot], s4.at[k, o - 1], r4.at[k, o - 1],
            device_id={"bl": peer}, device_id_type=MESH,
        )

    copies = []
    for k in range(2):
        for o in range(1, n):
            copy = deliver(k, o, flip(me, o, n), me)
            copy.start()
            copies.append(copy)
    got_b[me] = fit_out[me]
    got_g[me] = gains_send[me]
    for o in range(1, n):
        deliver(0, o, flip(me, o, n), flip(me, o, n)).wait_recv()
    total = got_b[0]
    for s in range(1, n):
        total = total + got_b[s]
    chunk_b[...] = total
    total = over_freq(chunk_b, got_fb, s5, r5)
    for o in range(1, n):
        deliver(1, o, flip(me, o, n), flip(me, o, n)).wait_recv()
    for copy in copies:
        copy.wait_send()
    for s in range(n):
        for a in range(2):
            for d in range(dirs):
                gains_ref[a, d, s * cl : (s + 1) * cl, :] = got_g[s, d * cl : (d + 1) * cl, a * owned : (a + 1) * owned]
    mine = basis_ref[me_f]
    for a in range(2):
        for d in range(dirs):
            value = None
            for j in range(JD):
                row = j * dirs + d
                term = mine[:, j : j + 1] * total[row : row + 1, a * owned : (a + 1) * owned]
                value = term if value is None else value + term
            cons_ref[a, d] = value


def calibrate(n, m, cl, rho, args, shape):
    coh, vis, gains, pairs = args[:4]
    rows = SKY_DIRECTIONS * cl
    hi = STATION_TOTAL // LO
    per = vis.shape[2]
    owned = STATION_TOTAL // n
    chunk = (JD * SKY_DIRECTIONS, 2 * owned)
    dma = pltpu.SemaphoreType.DMA
    vm = pltpu.VMEM
    return pl.pallas_call(
        functools.partial(calibrate_kernel, n, m, cl, rho),
        out_shape=[jax.ShapeDtypeStruct(shape, F32)] * 2,
        in_specs=[pl.BlockSpec(memory_space=pltpu.VMEM)] * len(args),
        out_specs=[pl.BlockSpec(memory_space=pltpu.VMEM)] * 2,
        scratch_shapes=[
            vm(coh.shape, coh.dtype), vm(vis.shape, vis.dtype), vm(gains.shape, F32), vm((n,) + pairs.shape, jnp.int32),
            vm((2, n, LO, per), BF16), vm((hi * 2 * rows, LO), BF16), vm((hi * 3 * rows, LO), F32),
            vm((n,) + chunk, F32), vm((n - 1,) + chunk, F32), vm(chunk, F32),
            vm((m - 1,) + chunk, F32), vm(chunk, F32), vm((n,) + chunk, F32),
            vm((n,) + chunk, F32), vm(gains.shape, F32), vm((n,) + chunk, F32), vm(gains.shape, F32),
            vm(chunk, F32), vm((m - 1,) + chunk, F32),
            dma((4, n - 1)), dma((4, n - 1)), dma((4,)),
            dma((n - 1,)), dma((n - 1,)), dma((m - 1,)), dma((m - 1,)), dma((n - 1,)), dma((n - 1,)),
            dma((2, n - 1)), dma((2, n - 1)), dma((m - 1,)), dma((m - 1,)),
        ],
        compiler_params=pltpu.CompilerParams(collective_id=0, has_side_effects=True, vmem_limit_bytes=VMEM_CAP),
    )(*args)


def shards(n, m, vis, coherency, gains_init, station_pairs):
    dirs = SKY_DIRECTIONS
    channels = vis.shape[1]
    per = vis.shape[2]
    owned = gains_init.shape[3]
    cl = channels // n
    rows = dirs * cl
    rho = 2.0 * per * n / STATION_TOTAL
    basis = basis_rows(channels * m)
    wide = np.zeros((m * n, 2, JD, dirs, 2, dirs, cl), np.float32)
    split = basis.reshape(JD, m * n, cl)
    for a in range(2):
        for d in range(dirs):
            wide[:, a, :, d, a, d, :] = np.moveaxis(split, 1, 0)
    wide = jnp.asarray(wide.reshape(m * n, JD * 2 * dirs, 2 * rows))
    basis_t = jnp.asarray(np.ascontiguousarray(basis.reshape(JD, m, channels).transpose(1, 2, 0)))

    coh_out = coherency.reshape(2, dirs, n, cl, per).transpose(2, 0, 1, 3, 4).reshape(n, 2, rows, per)
    vis_out = vis.reshape(2, n, cl, per).transpose(1, 0, 2, 3).reshape(n, 2 * cl, per)
    gains_out = gains_init.reshape(2, dirs, n, cl, owned).transpose(2, 1, 3, 0, 4).reshape(n, rows, 2 * owned)
    args = (coh_out, vis_out, gains_out, station_pairs, wide, basis_t)
    return tuple(calibrate(n, m, cl, rho, args, gains_init.shape))


def solution(mesh):
    placed = (
        P(None, "freq", "bl"),
        P(None, None, "freq", "bl"),
        P(None, None, "freq", "bl"),
        P(None, "bl"),
    )
    return jax.shard_map(
        functools.partial(shards, mesh.shape["bl"], mesh.shape["freq"]),
        mesh=mesh,
        in_specs=placed,
        out_specs=(P(None, None, "freq", "bl"), P(None, None, "freq", "bl")),
        check_vma=False,
    )
```

profile of v0, /device:TPU:0, one launch (start us, length us, event | category | flops | bytes accessed | tf_op | source)
XLA Modules:
  0.0 79.4 jit_solution(2885326350319240714)
XLA Ops:
  0.6 1.5 %reshape.22 = bf16[2,4,8,4,2048]{4,3,2,1,0:T(4,128)(2,1)S(1)} reshape(bf16[2,4,32,2048]{3,2,1,0:T(8,128)(2,1)} %param.7) | data formatting | bytes 2097152 | tf_op jit(solution)/shard_map/reshape | solution.py:369
  2.1 0.6 copy.14
  2.7 0.0 copy-start
  2.7 1.1 %reshape.23.coh_in = bf16[8,2,16,2048]{3,2,1,0:T(8,128)(2,1)} reshape(bf16[8,2,4,4,2048]{4,3,2,1,0:T(4,128)(2,1)S(1)} %bitcast.12) | data formatting | bytes 2097152 | tf_op jit(solution)/shard_map/reshape | solution.py:369
  3.8 0.0 copy-done
  3.8 0.1 reshape.24
  4.0 0.0 copy-start.1
  4.0 1.0 %reshape.25.vis_in = f32[8,8,2048]{2,1,0:T(8,128)} reshape(f32[8,2,4,2048]{3,2,1,0:T(4,128)S(1)} %bitcast.13) | data formatting | bytes 1048576 | tf_op jit(solution)/shard_map/reshape | solution.py:370
  5.0 0.0 copy-done.1
  5.0 0.1 copy.16
  5.1 0.8 reshape.27.gains_in
  5.9 71.2 %shard_map.77 = (f32[2,4,32,64]{3,2,1,0:T(8,128)}, f32[2,4,32,64]{3,2,1,0:T(8,128)}) custom-call(bf16[8,2,16,2048]{3,2,1,0:T(8,128)(2,1)} %reshape.23.coh_in, f32[8,8,2048]{2,1,0:T(8,128)} %reshape.25.vis_in, f32[8,16,128]{2,1,0:T(8,128)} %reshape.27.gains_in, s32[2,2048]{1,0:T(2,128)} %pairs_in.1, f32[32,32,32]{2,1,0:T(8,128)} %constant.4.clone.wide_ref, ...), custom_call_target="tpu_custom_call" | custom-call | tf_op jit(solution)/shard_map/pallas_call | solution.py:332
  77.1 0.0 copy-start.2
  77.1 1.6 %copy.19 = f32[2,4,32,64]{3,2,1,0:T(8,128)} copy(f32[2,4,32,64]{3,2,1,0:T(8,128)} %get-tuple-element.4) | data formatting | bytes 131072
  78.7 0.0 copy-done.2
  78.7 0.7 copy.20
  (1 shorter events, 0.0 us)
Async XLA Ops:
  2.7 1.1 %copy-start = (f32[2,32,2048]{2,1,0:T(8,128)S(1)}, f32[2,32,2048]{2,1,0:T(8,128)}, u32[]{:S(2)}) copy-start(f32[2,32,2048]{2,1,0:T(8,128)} %param.6) | copy-start | bytes 1572868
  4.0 1.0 %copy-start.1 = (f32[2,4,32,64]{3,2,1,0:T(8,128)S(1)}, f32[2,4,32,64]{3,2,1,0:T(8,128)}, u32[]{:S(2)}) copy-start(f32[2,4,32,64]{3,2,1,0:T(8,128)} %param.8) | copy-start | bytes 196612
  77.1 1.6 %copy-start.2 = (f32[2,4,32,64]{3,2,1,0:T(8,128)S(1)}, f32[2,4,32,64]{3,2,1,0:T(8,128)}, u32[]{:S(2)}) copy-start(f32[2,4,32,64]{3,2,1,0:T(8,128)} %get-tuple-element.5) | copy-start | bytes 196612
where the time goes:
time: 79.6 us; the launch traced here: 79.4 us
  Pallas kernels  71.2 us (89%)
  local copies, waits for them, and re-layouts  7.46 us (9%)
    pallas_call x1, Pallas kernels, calibrate(): pl.pallas_call(functools.partial(calibrate_kernel, n, m, cl, rho), out_sh...  71.2 us
    reshape x3, local copies, waits for them, and re-layouts, shards(): coherency.reshape(2, dirs, n, cl, per).transpose(2, 0, 1, 3, 4)  3.15 us
    unnamed x8, local copies, waits for them, and re-layouts  2.28 us

commit v1 on v0

--- a/solution.py
+++ b/solution.py
@@ -154,7 +154,7 @@
         xi = nr * ci + ni * cr
         mr = sum_directions(nr * zr - ni * zi, cl)
         mi = sum_directions(nr * zi + ni * zr, cl)
-        v = vis_all[block]
+        v = vis_all[block].astype(F32)
         rr = jnp.concatenate([v[:cl]] * dirs, axis=0) - mr
         ri = jnp.concatenate([v[cl:]] * dirs, axis=0) - mi
         t1 = spread([rr * zr + ri * zi, ri * zr - rr * zi, zr * zr + zi * zi], group0)
@@ -189,7 +189,7 @@
         half = x.shape[0] // 2
         return jnp.concatenate([x[:half, s * owned : (s + 1) * owned], x[half:, s * owned : (s + 1) * owned]], axis=1)
 
-    def over_freq(src, slots, send, recv):
+    def start_freq(src, slots, send, recv):
         copies = []
         for o in range(1, m):
             copy = pltpu.make_async_remote_copy(
@@ -198,7 +198,9 @@
             )
             copy.start()
             copies.append(copy)
-        total = src[...]
+        return copies
+
+    def sum_freq(copies, total, slots):
         for o in range(1, m):
             copies[o - 1].wait()
             total = total + slots[o - 1]
@@ -239,12 +241,17 @@
         )
         copy.start()
         copies.append(copy)
+    load_table(gains)
+    cut = (n * 3 // 8, n * 6 // 8)
+    lax.fori_loop(0, cut[0], again, 0)
     total = part[me]
     for o in range(1, n):
         copies[o - 1].wait()
         total = total + got[o - 1]
     chunk[...] = total
-    total = over_freq(chunk, got_f, s2, r2)
+    copies = start_freq(chunk, got_f, s2, r2)
+    lax.fori_loop(cut[0], cut[1], again, 0)
+    total = sum_freq(copies, total, got_f)
     whole[...] = total
     copies = []
     for o in range(1, n):
@@ -255,6 +262,7 @@
         copy.start()
         copies.append(copy)
     coef[me] = total
+    lax.fori_loop(cut[1], n, again, 0)
     for copy in copies:
         copy.wait_send()
     for o in range(1, n):
@@ -269,7 +277,8 @@
     )
     dual = gains - consensus
     target = consensus - dual
-    for _ in range(ITERS):
+    gains = advance(gains, target)
+    for _ in range(ITERS - 1):
         load_table(gains)
         lax.fori_loop(0, n, again, 0)
         gains = advance(gains, target)
@@ -300,7 +309,7 @@
     for s in range(1, n):
         total = total + got_b[s]
     chunk_b[...] = total
-    total = over_freq(chunk_b, got_fb, s5, r5)
+    total = sum_freq(start_freq(chunk_b, got_fb, s5, r5), total, got_fb)
     for o in range(1, n):
         deliver(1, o, flip(me, o, n), flip(me, o, n)).wait_recv()
     for copy in copies:
@@ -367,7 +376,7 @@
     basis_t = jnp.asarray(np.ascontiguousarray(basis.reshape(JD, m, channels).transpose(1, 2, 0)))
 
     coh_out = coherency.reshape(2, dirs, n, cl, per).transpose(2, 0, 1, 3, 4).reshape(n, 2, rows, per)
-    vis_out = vis.reshape(2, n, cl, per).transpose(1, 0, 2, 3).reshape(n, 2 * cl, per)
+    vis_out = vis.reshape(2, n, cl, per).transpose(1, 0, 2, 3).reshape(n, 2 * cl, per).astype(BF16)
     gains_out = gains_init.reshape(2, dirs, n, cl, owned).transpose(2, 1, 3, 0, 4).reshape(n, rows, 2 * owned)
     args = (coh_out, vis_out, gains_out, station_pairs, wide, basis_t)
     return tuple(calibrate(n, m, cl, rho, args, gains_init.shape))

time: 79.6 us -> 69.5 us (0.87)
  Pallas kernels: 71.2 us -> 61.2 us
    pallas_call x1, Pallas kernels: 71.2 us -> 61.2 us  [calibrate(): pl.pallas_call(functools.partial(calibrate_kernel, n, m, cl, rho), out_sh...]
    reshape x3 -> x0, local copies, waits for them, and re-layouts: 1.18 us -> none  [shards(): vis.reshape(2, n, cl, per).transpose(1, 0, 2, 3).reshape(n, 2 * cl, per)]
    convert_element_type x0 -> x3, local copies, waits for them, and re-layouts: none -> 0.97 us  [shards(): vis.reshape(2, n, cl, per).transpose(1, 0, 2, 3).reshape(n, 2 * cl, per)]
where the time goes in v1:
time: 69.5 us; the launch traced here: 69.3 us
  Pallas kernels  61.2 us (88%)
  local copies, waits for them, and re-layouts  7.38 us (11%)
  between operations  0.7 us (1%)
    pallas_call x1, Pallas kernels, calibrate(): pl.pallas_call(functools.partial(calibrate_kernel, n, m, cl, rho), out_sh...  61.2 us
    reshape x3, local copies, waits for them, and re-layouts, shards(): coherency.reshape(2, dirs, n, cl, per).transpose(2, 0, 1, 3, 4)  3.15 us
    unnamed x8, local copies, waits for them, and re-layouts  2.4 us

profile of v1, /device:TPU:0, one launch (start us, length us, event | category | flops | bytes accessed | tf_op | source)
XLA Modules:
  0.0 69.3 jit_solution(2985941514681255542)
XLA Ops:
  0.6 1.5 %reshape.20 = bf16[2,4,8,4,2048]{4,3,2,1,0:T(4,128)(2,1)S(1)} reshape(bf16[2,4,32,2048]{3,2,1,0:T(8,128)(2,1)} %param.7) | data formatting | bytes 2097152 | tf_op jit(solution)/shard_map/reshape | solution.py:378
  2.1 0.6 copy.14
  2.7 0.0 copy-start
  2.7 1.1 %reshape.21.coh_in = bf16[8,2,16,2048]{3,2,1,0:T(8,128)(2,1)} reshape(bf16[8,2,4,4,2048]{4,3,2,1,0:T(4,128)(2,1)S(1)} %bitcast.12) | data formatting | bytes 2097152 | tf_op jit(solution)/shard_map/reshape | solution.py:378
  3.8 0.0 copy-done
  3.8 0.1 convert_element_type.10
  3.9 0.1 copy.15
  4.1 0.0 copy-start.1
  4.1 0.8 %convert_element_type.12.vis_in = bf16[8,8,2048]{2,1,0:T(8,128)(2,1)} reshape(bf16[8,2,4,2048]{3,2,1,0:T(4,128)(2,1)S(1)} %bitcast.13) | data formatting | bytes 524288 | tf_op jit(solution)/shard_map/convert_element_type | solution.py:379
  4.8 0.1 copy-done.1
  5.0 0.1 copy.16
  5.1 0.8 %reshape.23.gains_in = f32[8,16,128]{2,1,0:T(8,128)} reshape(f32[8,4,4,2,64]{4,3,2,1,0:T(2,128)S(1)} %bitcast.14) | data formatting | bytes 131072 | tf_op jit(solution)/shard_map/reshape | solution.py:380
  5.8 61.2 %shard_map.77 = (f32[2,4,32,64]{3,2,1,0:T(8,128)}, f32[2,4,32,64]{3,2,1,0:T(8,128)}) custom-call(bf16[8,2,16,2048]{3,2,1,0:T(8,128)(2,1)} %reshape.21.coh_in, bf16[8,8,2048]{2,1,0:T(8,128)(2,1)} %convert_element_type.12.vis_in, f32[8,16,128]{2,1,0:T(8,128)} %reshape.23.gains_in, s32[2,2048]{1,0:T(2,128)} %pairs_in.1, f32[32,32,32]{2,1,0:T(8,128)} %constant.4.clone.wide_ref, ...), custom_call_target="tpu_custom_call" | custom-call | tf_op jit(solution)/shard_map/pallas_call | solution.py:341
  67.0 0.0 copy-start.2
  67.0 1.6 %copy.19 = f32[2,4,32,64]{3,2,1,0:T(8,128)} copy(f32[2,4,32,64]{3,2,1,0:T(8,128)} %get-tuple-element.4) | data formatting | bytes 131072
  68.6 0.0 copy-done.2
  68.6 0.7 copy.20
  (1 shorter events, 0.0 us)
Async XLA Ops:
  2.7 1.1 %copy-start = (f32[2,32,2048]{2,1,0:T(8,128)S(1)}, f32[2,32,2048]{2,1,0:T(8,128)}, u32[]{:S(2)}) copy-start(f32[2,32,2048]{2,1,0:T(8,128)} %param.6) | copy-start | bytes 1572868
  4.1 0.9 %copy-start.1 = (f32[2,4,32,64]{3,2,1,0:T(8,128)S(1)}, f32[2,4,32,64]{3,2,1,0:T(8,128)}, u32[]{:S(2)}) copy-start(f32[2,4,32,64]{3,2,1,0:T(8,128)} %param.8) | copy-start | bytes 196612
  67.0 1.6 %copy-start.2 = (f32[2,4,32,64]{3,2,1,0:T(8,128)S(1)}, f32[2,4,32,64]{3,2,1,0:T(8,128)}, u32[]{:S(2)}) copy-start(f32[2,4,32,64]{3,2,1,0:T(8,128)} %get-tuple-element.5) | copy-start | bytes 196612

commit v2 on v1

--- a/solution.py
+++ b/solution.py
@@ -18,6 +18,8 @@
 F32 = jnp.float32
 BF16 = jnp.bfloat16
 LO = 128
+VIS_TOP = 60.0
+VIS_STEPS = 32767.0
 VMEM_CAP = 60 * 1024 * 1024
 
 
@@ -34,14 +36,16 @@
 
 def greet(axes):
     barrier = pltpu.get_barrier_semaphore()
-    count = 0
     for axis in axes:
         n = lax.axis_size(axis)
         me = lax.axis_index(axis)
         for o in range(1, n):
             pl.semaphore_signal(barrier, inc=1, device_id={axis: lax.rem(me + o, n)}, device_id_type=MESH)
-            count += 1
-    pl.semaphore_wait(barrier, count)
+
+
+def meet(axes):
+    count = sum(lax.axis_size(axis) - 1 for axis in axes)
+    pl.semaphore_wait(pltpu.get_barrier_semaphore(), count)
 
 
 def sum_directions(x, cl):
@@ -68,29 +72,61 @@
 
 def calibrate_kernel(
     n, m, cl, rho,
-    coh_in, vis_in, gains_in, pairs_in, wide_ref, basis_ref,
+    coh_raw, vis_raw, gains_raw, pairs_in, wide_raw, basis_raw,
     gains_ref, cons_ref,
+    coh_own, vis_own, gains_own, wide_ref, basis_ref, coh_send, vis_send,
     coh_all, vis_all, gains_all, pairs_all, onehot, table, acc,
     part, got, chunk, got_f, whole, coef, fit_out, gains_send, got_b, got_g, chunk_b, got_fb,
-    sx, rx, lx, s1, r1, s2, r2, s3, r3, s4, r4, s5, r5,
+    lr, sx, rx, lx, s1, r1, s2, r2, s3, r3, s4, r4, s5, r5,
 ):
     dirs = SKY_DIRECTIONS
     rows = dirs * cl
     lo = LO
     hi = STATION_TOTAL // lo
-    per = vis_in.shape[2]
+    per = vis_raw.shape[2]
     owned = STATION_TOTAL // n
     me = lax.axis_index("bl")
     me_f = lax.axis_index("freq")
     greet(("bl", "freq"))
+    loads = [
+        pltpu.make_async_copy(gains_raw, gains_own, lr.at[0]),
+        pltpu.make_async_copy(coh_raw, coh_own, lr.at[1]),
+        pltpu.make_async_copy(vis_raw, vis_own, lr.at[2]),
+        pltpu.make_async_copy(wide_raw.at[me_f * n + me], wide_ref, lr.at[3]),
+        pltpu.make_async_copy(basis_raw.at[me_f], basis_ref, lr.at[4]),
+    ]
+    for copy in loads:
+        copy.start()
 
     def transfer(a, o, peer, src, slot):
-        ref = (gains_in, pairs_in, coh_in, vis_in)[a]
+        ref = (gains_send, pairs_in, coh_send, vis_send)[a]
         dst = (gains_all, pairs_all, coh_all, vis_all)[a]
         return pltpu.make_async_remote_copy(
             ref if a == 1 else ref.at[src], dst.at[slot], sx.at[a, o - 1], rx.at[a, o - 1],
             device_id={"bl": peer}, device_id_type=MESH,
         )
+
+    def of(x, s):
+        return x[s * cl : (s + 1) * cl]
+
+    loads[0].wait()
+    parts = [[gains_own[a, d] for d in range(dirs)] for a in range(2)]
+    for s in range(n):
+        gains_send[s] = jnp.concatenate(
+            [jnp.concatenate([of(x, s) for x in parts[a]], axis=0) for a in range(2)], axis=1
+        )
+    loads[1].wait()
+    for a in range(2):
+        parts = [coh_own[a, d].astype(F32) for d in range(dirs)]
+        for s in range(n):
+            coh_send[s, a] = jnp.concatenate([of(x, s) for x in parts], axis=0).astype(BF16)
+    loads[2].wait()
+    parts = [jnp.round(vis_own[a] * (VIS_STEPS / VIS_TOP)).astype(jnp.int32) for a in range(2)]
+    for s in range(n):
+        vis_send[s] = jnp.concatenate([of(x, s) for x in parts], axis=0).astype(jnp.int16)
+    for copy in loads[3:]:
+        copy.wait()
+    meet(("bl", "freq"))
 
     sends = []
     for group in ((0, 1), (2, 3)):
@@ -101,10 +137,10 @@
                 copy.start()
                 sends.append(copy)
     own = [
-        pltpu.make_async_copy(gains_in.at[me], gains_all.at[me], lx.at[0]),
+        pltpu.make_async_copy(gains_send.at[me], gains_all.at[me], lx.at[0]),
         pltpu.make_async_copy(pairs_in, pairs_all.at[me], lx.at[1]),
-        pltpu.make_async_copy(coh_in.at[me], coh_all.at[me], lx.at[2]),
-        pltpu.make_async_copy(vis_in.at[me], vis_all.at[me], lx.at[3]),
+        pltpu.make_async_copy(coh_send.at[me], coh_all.at[me], lx.at[2]),
+        pltpu.make_async_copy(vis_send.at[me], vis_all.at[me], lx.at[3]),
     ]
     for copy in own:
         copy.start()
@@ -113,7 +149,7 @@
     for o in range(1, n):
         transfer(0, o, flip(me, o, n), me, flip(me, o, n)).wait_recv()
 
-    wide = wide_ref[me_f * n + me]
+    wide = wide_ref[...]
 
     def build(block):
         station = lax.broadcasted_iota(jnp.int32, (lo, per), 0)
@@ -154,7 +190,7 @@
         xi = nr * ci + ni * cr
         mr = sum_directions(nr * zr - ni * zi, cl)
         mi = sum_directions(nr * zi + ni * zr, cl)
-        v = vis_all[block].astype(F32)
+        v = vis_all[block].astype(jnp.int32).astype(F32) * (VIS_TOP / VIS_STEPS)
         rr = jnp.concatenate([v[:cl]] * dirs, axis=0) - mr
         ri = jnp.concatenate([v[cl:]] * dirs, axis=0) - mi
         t1 = spread([rr * zr + ri * zi, ri * zr - rr * zi, zr * zr + zi * zi], group0)
@@ -318,7 +354,7 @@
         for a in range(2):
             for d in range(dirs):
                 gains_ref[a, d, s * cl : (s + 1) * cl, :] = got_g[s, d * cl : (d + 1) * cl, a * owned : (a + 1) * owned]
-    mine = basis_ref[me_f]
+    mine = basis_ref[...]
     for a in range(2):
         for d in range(dirs):
             value = None
@@ -330,27 +366,32 @@
 
 
 def calibrate(n, m, cl, rho, args, shape):
-    coh, vis, gains, pairs = args[:4]
+    coh, vis, gains, pairs, wide, basis = args
     rows = SKY_DIRECTIONS * cl
     hi = STATION_TOTAL // LO
     per = vis.shape[2]
     owned = STATION_TOTAL // n
+    coh_split = (n, 2, rows, per)
+    vis_split = (n, 2 * cl, per)
+    gains_split = (n, rows, 2 * owned)
     chunk = (JD * SKY_DIRECTIONS, 2 * owned)
     dma = pltpu.SemaphoreType.DMA
     vm = pltpu.VMEM
     return pl.pallas_call(
         functools.partial(calibrate_kernel, n, m, cl, rho),
         out_shape=[jax.ShapeDtypeStruct(shape, F32)] * 2,
-        in_specs=[pl.BlockSpec(memory_space=pltpu.VMEM)] * len(args),
+        in_specs=[pl.BlockSpec(memory_space=pl.ANY)] * len(args),
         out_specs=[pl.BlockSpec(memory_space=pltpu.VMEM)] * 2,
         scratch_shapes=[
-            vm(coh.shape, coh.dtype), vm(vis.shape, vis.dtype), vm(gains.shape, F32), vm((n,) + pairs.shape, jnp.int32),
+            vm(coh.shape, coh.dtype), vm(vis.shape, F32), vm(gains.shape, F32), vm(wide.shape[1:], F32),
+            vm(basis.shape[1:], F32), vm(coh_split, BF16), vm(vis_split, jnp.int16),
+            vm(coh_split, BF16), vm(vis_split, jnp.int16), vm(gains_split, F32), vm((n,) + pairs.shape, jnp.int32),
             vm((2, n, LO, per), BF16), vm((hi * 2 * rows, LO), BF16), vm((hi * 3 * rows, LO), F32),
             vm((n,) + chunk, F32), vm((n - 1,) + chunk, F32), vm(chunk, F32),
             vm((m - 1,) + chunk, F32), vm(chunk, F32), vm((n,) + chunk, F32),
-            vm((n,) + chunk, F32), vm(gains.shape, F32), vm((n,) + chunk, F32), vm(gains.shape, F32),
+            vm((n,) + chunk, F32), vm(gains_split, F32), vm((n,) + chunk, F32), vm(gains_split, F32),
             vm(chunk, F32), vm((m - 1,) + chunk, F32),
-            dma((4, n - 1)), dma((4, n - 1)), dma((4,)),
+            dma((5,)), dma((4, n - 1)), dma((4, n - 1)), dma((4,)),
             dma((n - 1,)), dma((n - 1,)), dma((m - 1,)), dma((m - 1,)), dma((n - 1,)), dma((n - 1,)),
             dma((2, n - 1)), dma((2, n - 1)), dma((m - 1,)), dma((m - 1,)),
         ],
@@ -375,10 +416,7 @@
     wide = jnp.asarray(wide.reshape(m * n, JD * 2 * dirs, 2 * rows))
     basis_t = jnp.asarray(np.ascontiguousarray(basis.reshape(JD, m, channels).transpose(1, 2, 0)))
 
-    coh_out = coherency.reshape(2, dirs, n, cl, per).transpose(2, 0, 1, 3, 4).reshape(n, 2, rows, per)
-    vis_out = vis.reshape(2, n, cl, per).transpose(1, 0, 2, 3).reshape(n, 2 * cl, per).astype(BF16)
-    gains_out = gains_init.reshape(2, dirs, n, cl, owned).transpose(2, 1, 3, 0, 4).reshape(n, rows, 2 * owned)
-    args = (coh_out, vis_out, gains_out, station_pairs, wide, basis_t)
+    args = (coherency, vis, gains_init, station_pairs, wide, basis_t)
     return tuple(calibrate(n, m, cl, rho, args, gains_init.shape))
 
 

time: 69.5 us -> 63 us (0.906)
  local copies, waits for them, and re-layouts: 7.38 us -> 2.26 us
  Pallas kernels: 61.2 us -> 59.9 us
    reshape x5 -> x0, local copies, waits for them, and re-layouts: 4.01 us -> none  [the longest x3 3.15 us: shards(): coherency.reshape(2, dirs, n, cl, per).transpose(2, 0, 1, 3, 4)]
    pallas_call x1, Pallas kernels: 61.2 us -> 59.9 us  [calibrate(): pl.pallas_call(functools.partial(calibrate_kernel, n, m, cl, rho), out_sh...]
    convert_element_type x3 -> x0, local copies, waits for them, and re-layouts: 0.97 us -> none  [shards(): vis.reshape(2, n, cl, per).transpose(1, 0, 2, 3).reshape(n, 2 * cl, per)]
    unnamed x8 -> x4, local copies, waits for them, and re-layouts: 2.4 us -> 2.26 us
where the time goes in v2:
time: 63 us; the launch traced here: 62.8 us
  Pallas kernels  59.9 us (95%)
  local copies, waits for them, and re-layouts  2.26 us (4%)
  between operations  0.65 us (1%)
    pallas_call x1, Pallas kernels, calibrate(): pl.pallas_call(functools.partial(calibrate_kernel, n, m, cl, rho), out_sh...  59.9 us
    unnamed x4, local copies, waits for them, and re-layouts  2.26 us

profile of v2, /device:TPU:0, one launch (start us, length us, event | category | flops | bytes accessed | tf_op | source)
XLA Modules:
  0.0 62.8 jit_solution(6745571394919158838)
XLA Ops:
  0.6 59.9 %shard_map.77 = (f32[2,4,32,64]{3,2,1,0:T(8,128)}, f32[2,4,32,64]{3,2,1,0:T(8,128)}) custom-call(bf16[2,4,32,2048]{3,2,1,0:T(8,128)(2,1)} %coh_raw.1, f32[2,32,2048]{2,1,0:T(8,128)} %vis_raw.1, f32[2,4,32,64]{3,2,1,0:T(8,128)} %gains_raw.1, s32[2,2048]{1,0:T(2,128)} %pairs_in.1, f32[32,32,32]{2,1,0:T(8,128)} %constant.4.clone.wide_raw, ...), custom_call_target="tpu_custom_call" | custom-call | tf_op jit(solution)/shard_map/pallas_call | solution.py:380
  60.5 0.0 copy-start
  60.5 1.6 %copy.10 = f32[2,4,32,64]{3,2,1,0:T(8,128)} copy(f32[2,4,32,64]{3,2,1,0:T(8,128)} %get-tuple-element.4) | data formatting | bytes 131072
  62.1 0.0 copy-done
  62.1 0.7 %copy.11 = f32[2,4,32,64]{3,2,1,0:T(8,128)} copy(f32[2,4,32,64]{3,2,1,0:T(8,128)S(1)} %copy-done) | data formatting | bytes 131072
Async XLA Ops:
  60.5 1.6 %copy-start = (f32[2,4,32,64]{3,2,1,0:T(8,128)S(1)}, f32[2,4,32,64]{3,2,1,0:T(8,128)}, u32[]{:S(2)}) copy-start(f32[2,4,32,64]{3,2,1,0:T(8,128)} %get-tuple-element.5) | copy-start | bytes 196612

commit v3 on v2

--- a/solution.py
+++ b/solution.py
@@ -18,6 +18,7 @@
 F32 = jnp.float32
 BF16 = jnp.bfloat16
 LO = 128
+LO_SUM = 256
 VIS_TOP = 60.0
 VIS_STEPS = 32767.0
 VMEM_CAP = 60 * 1024 * 1024
@@ -75,7 +76,7 @@
     coh_raw, vis_raw, gains_raw, pairs_in, wide_raw, basis_raw,
     gains_ref, cons_ref,
     coh_own, vis_own, gains_own, wide_ref, basis_ref, coh_send, vis_send,
-    coh_all, vis_all, gains_all, pairs_all, onehot, table, acc,
+    coh_all, vis_all, gains_all, pairs_all, onehot, upright, table, held, acc,
     part, got, chunk, got_f, whole, coef, fit_out, gains_send, got_b, got_g, chunk_b, got_fb,
     lr, sx, rx, lx, s1, r1, s2, r2, s3, r3, s4, r4, s5, r5,
 ):
@@ -84,6 +85,8 @@
     lo = LO
     hi = STATION_TOTAL // lo
     per = vis_raw.shape[2]
+    los = acc.shape[1]
+    his = STATION_TOTAL // los
     owned = STATION_TOTAL // n
     me = lax.axis_index("bl")
     me_f = lax.axis_index("freq")
@@ -156,6 +159,14 @@
         for t in range(2):
             index = pairs_all[block, t : t + 1, :] & (lo - 1)
             onehot[t, block] = jnp.where(station == index, 1.0, 0.0).astype(BF16)
+            if los == lo:
+                continue
+            lanes = lax.broadcasted_iota(jnp.int32, (lo, los), 1)
+            for p in range(per // lo):
+                row = pairs_all[block, t : t + 1, p * lo : (p + 1) * lo] & (los - 1)
+                column = jnp.transpose(jnp.broadcast_to(row, (lo, lo)))
+                column = jnp.concatenate([column] * (los // lo), axis=1)
+                upright[t, block, p * lo : (p + 1) * lo] = jnp.where(lanes == column, 1.0, 0.0).astype(BF16)
 
     def pick(x, group):
         value = x[: 2 * rows]
@@ -163,23 +174,47 @@
             value = jnp.where(group == h, x[2 * rows * h : 2 * rows * (h + 1)], value)
         return value
 
+    def looked_up(block, t, at):
+        row = pairs_all[block, t : t + 1, at : at + lo]
+        index = jnp.broadcast_to(row & (lo - 1), (8, lo))
+        group = jnp.broadcast_to(lax.shift_right_logical(row, lo.bit_length() - 1), (8, lo))
+        out = []
+        for r in range(0, 2 * rows, 8):
+            value = None
+            for h in range(hi):
+                found = jnp.take_along_axis(held[h, r : r + 8], index, axis=1, mode="promise_in_bounds")
+                value = found if value is None else jnp.where(group == h, found, value)
+            out.append(value)
+        return jnp.concatenate(out, axis=0)
+
+    def gather(block, t, group, tiles):
+        parts = [looked_up(block, t, p * lo) for p in range(tiles)]
+        if tiles * lo < per:
+            ahead = tiles * lo
+            parts.append(
+                pick(
+                    jnp.dot(table[...], onehot[t, block, :, ahead:], preferred_element_type=F32), group[:, ahead:]
+                )
+            )
+        return jnp.concatenate(parts, axis=1)
+
     def spread(terms, group):
         terms = jnp.concatenate(terms, axis=0).astype(BF16)
         return jnp.concatenate(
             [
-                terms * jnp.broadcast_to(jnp.where(group == h, 1.0, 0.0), (3 * rows, per)).astype(BF16)
-                for h in range(hi)
+                terms * jnp.broadcast_to(jnp.where(group == h, 1.0, 0.0), terms.shape).astype(BF16)
+                for h in range(his)
             ],
             axis=0,
         )
 
-    def add_block(block):
+    def sums_of(block):
         group0 = lax.shift_right_logical(pairs_all[block, 0:1, :], lo.bit_length() - 1)
         group1 = lax.shift_right_logical(pairs_all[block, 1:2, :], lo.bit_length() - 1)
         ohn = onehot[0, block]
         ohf = onehot[1, block]
-        near = pick(jnp.dot(table[...], ohn, preferred_element_type=F32), group0)
-        far = pick(jnp.dot(table[...], ohf, preferred_element_type=F32), group1)
+        near = gather(block, 0, group0, min(16, per // lo))
+        far = gather(block, 1, group1, min(0, per // lo))
         nr, ni = near[:rows], near[rows:]
         fr, fi = far[:rows], far[rows:]
         cr = coh_all[block, 0].astype(F32)
@@ -193,26 +228,35 @@
         v = vis_all[block].astype(jnp.int32).astype(F32) * (VIS_TOP / VIS_STEPS)
         rr = jnp.concatenate([v[:cl]] * dirs, axis=0) - mr
         ri = jnp.concatenate([v[cl:]] * dirs, axis=0) - mi
-        t1 = spread([rr * zr + ri * zi, ri * zr - rr * zi, zr * zr + zi * zi], group0)
-        t2 = spread([rr * xr + ri * xi, rr * xi - ri * xr, xr * xr + xi * xi], group1)
+        t1 = spread([rr * zr + ri * zi, ri * zr - rr * zi, zr * zr + zi * zi], lax.shift_right_logical(pairs_all[block, 0:1, :], los.bit_length() - 1))
+        t2 = spread([rr * xr + ri * xi, rr * xi - ri * xr, xr * xr + xi * xi], lax.shift_right_logical(pairs_all[block, 1:2, :], los.bit_length() - 1))
+        if los > lo:
+            return jnp.dot(t1, upright[0, block], preferred_element_type=F32) + jnp.dot(
+                t2, upright[1, block], preferred_element_type=F32
+            )
         contract = (((1,), (1,)), ((), ()))
-        acc[...] += lax.dot_general(t1, ohn, contract, preferred_element_type=F32) + lax.dot_general(
+        return lax.dot_general(t1, ohn, contract, preferred_element_type=F32) + lax.dot_general(
             t2, ohf, contract, preferred_element_type=F32
         )
+
+    def add_block(block):
+        acc[...] += sums_of(block)
 
     def load_table(gains):
         rounded = gains.astype(BF16)
+        for h in range(hi):
+            held[h] = rounded[:, h * lo : (h + 1) * lo].astype(F32)
         table[...] = jnp.concatenate([rounded[:, h * lo : (h + 1) * lo] for h in range(hi)], axis=0)
         acc[...] = jnp.zeros_like(acc)
 
     def advance(gains, target):
-        sums = jnp.concatenate([acc[3 * rows * h : 3 * rows * (h + 1)] for h in range(hi)], axis=1)
+        sums = jnp.concatenate([acc[3 * rows * h : 3 * rows * (h + 1)] for h in range(his)], axis=1)
         below = 2.0 * sums[2 * rows :] + rho
         below = jnp.concatenate([below, below], axis=0)
         return gains + (sums[: 2 * rows] + rho * (target - gains)) / below
 
     def again(block, carry):
-        add_block(block)
+        acc[...] += sums_of(2 * block) + sums_of(2 * block + 1)
         return carry
 
     def whole_rows(ref):
@@ -248,19 +292,25 @@
 
     def arriving(o, carry):
         peer = flip(me, o, n)
-        for a in (1, 2, 3):
+        for a in (2, 3):
             transfer(a, o, peer, me, peer).wait_recv()
-        build(peer)
         add_block(peer)
         return carry
 
+    def known(o, carry):
+        peer = flip(me, o, n)
+        transfer(1, o, peer, me, peer).wait_recv()
+        build(peer)
+        return carry
+
     build(me)
     add_block(me)
+    lax.fori_loop(1, n, known, 0)
     lax.fori_loop(1, n, arriving, 0)
     gains = advance(gains, target)
     for _ in range(ITERS - 1):
         load_table(gains)
-        lax.fori_loop(0, n, again, 0)
+        lax.fori_loop(0, n // 2, again, 0)
         gains = advance(gains, target)
     for copy in sends:
         copy.wait_send()
@@ -278,7 +328,7 @@
         copy.start()
         copies.append(copy)
     load_table(gains)
-    cut = (n * 3 // 8, n * 6 // 8)
+    cut = (n // 8, n * 3 // 8)
     lax.fori_loop(0, cut[0], again, 0)
     total = part[me]
     for o in range(1, n):
@@ -298,7 +348,7 @@
         copy.start()
         copies.append(copy)
     coef[me] = total
-    lax.fori_loop(cut[1], n, again, 0)
+    lax.fori_loop(cut[1], n // 2, again, 0)
     for copy in copies:
         copy.wait_send()
     for o in range(1, n):
@@ -316,7 +366,7 @@
     gains = advance(gains, target)
     for _ in range(ITERS - 1):
         load_table(gains)
-        lax.fori_loop(0, n, again, 0)
+        lax.fori_loop(0, n // 2, again, 0)
         gains = advance(gains, target)
 
     fitted = jnp.dot(wide, gains + dual, precision=HIGH, preferred_element_type=F32)
@@ -371,6 +421,8 @@
     hi = STATION_TOTAL // LO
     per = vis.shape[2]
     owned = STATION_TOTAL // n
+    los = LO_SUM if n * per <= 16384 else LO
+    tall = (2, n, per, los) if los > LO else (8, LO)
     coh_split = (n, 2, rows, per)
     vis_split = (n, 2 * cl, per)
     gains_split = (n, rows, 2 * owned)
@@ -386,7 +438,8 @@
             vm(coh.shape, coh.dtype), vm(vis.shape, F32), vm(gains.shape, F32), vm(wide.shape[1:], F32),
             vm(basis.shape[1:], F32), vm(coh_split, BF16), vm(vis_split, jnp.int16),
             vm(coh_split, BF16), vm(vis_split, jnp.int16), vm(gains_split, F32), vm((n,) + pairs.shape, jnp.int32),
-            vm((2, n, LO, per), BF16), vm((hi * 2 * rows, LO), BF16), vm((hi * 3 * rows, LO), F32),
+            vm((2, n, LO, per), BF16), vm(tall, BF16), vm((hi * 2 * rows, LO), BF16),
+            vm((hi, 2 * rows, LO), F32), vm((STATION_TOTAL // los * 3 * rows, los), F32),
             vm((n,) + chunk, F32), vm((n - 1,) + chunk, F32), vm(chunk, F32),
             vm((m - 1,) + chunk, F32), vm(chunk, F32), vm((n,) + chunk, F32),
             vm((n,) + chunk, F32), vm(gains_split, F32), vm((n,) + chunk, F32), vm(gains_split, F32),

time: 63 us -> 60.1 us (0.954)
  Pallas kernels: 59.9 us -> 56.9 us
    pallas_call x1, Pallas kernels: 59.9 us -> 56.9 us  [calibrate(): pl.pallas_call(functools.partial(calibrate_kernel, n, m, cl, rho), out_sh...]
where the time goes in v3:
time: 60.1 us; the launch traced here: 59.8 us
  Pallas kernels  56.9 us (95%)
  local copies, waits for them, and re-layouts  2.26 us (4%)
  between operations  0.65 us (1%)
    pallas_call x1, Pallas kernels, calibrate(): pl.pallas_call(functools.partial(calibrate_kernel, n, m, cl, rho), out_sh...  56.9 us
    unnamed x4, local copies, waits for them, and re-layouts  2.26 us

profile of v3, /device:TPU:0, one launch (start us, length us, event | category | flops | bytes accessed | tf_op | source)
XLA Modules:
  0.0 59.8 jit_solution(13754935269627476053)
XLA Ops:
  0.6 56.9 %shard_map.77 = (f32[2,4,32,64]{3,2,1,0:T(8,128)}, f32[2,4,32,64]{3,2,1,0:T(8,128)}) custom-call(bf16[2,4,32,2048]{3,2,1,0:T(8,128)(2,1)} %coh_raw.1, f32[2,32,2048]{2,1,0:T(8,128)} %vis_raw.1, f32[2,4,32,64]{3,2,1,0:T(8,128)} %gains_raw.1, s32[2,2048]{1,0:T(2,128)} %pairs_in.1, f32[32,32,32]{2,1,0:T(8,128)} %constant.4.clone.wide_raw, ...), custom_call_target="tpu_custom_call" | custom-call | tf_op jit(solution)/shard_map/pallas_call | solution.py:432
  57.6 0.0 copy-start
  57.6 1.6 %copy.10 = f32[2,4,32,64]{3,2,1,0:T(8,128)} copy(f32[2,4,32,64]{3,2,1,0:T(8,128)} %get-tuple-element.4) | data formatting | bytes 131072
  59.2 0.0 copy-done
  59.2 0.7 %copy.11 = f32[2,4,32,64]{3,2,1,0:T(8,128)} copy(f32[2,4,32,64]{3,2,1,0:T(8,128)S(1)} %copy-done) | data formatting | bytes 131072
Async XLA Ops:
  57.6 1.6 %copy-start = (f32[2,4,32,64]{3,2,1,0:T(8,128)S(1)}, f32[2,4,32,64]{3,2,1,0:T(8,128)}, u32[]{:S(2)}) copy-start(f32[2,4,32,64]{3,2,1,0:T(8,128)} %get-tuple-element.5) | copy-start | bytes 196612
